TPU v7x, 32 devices: a whole 2x2x4 slice. The times are simulated.
32 devices in a mesh: groups: 1, ctx: 16 (over z, y, x), tp: 2 (over core).
Axes of the slice: x: 2, y: 2, z: 4, core: 2. Of those that a mesh axis runs over, the one named last changes fastest.
Arguments:
- queries: bfloat16 [4, 32, 64, 128], P('groups', 'ctx', 'tp'), may hold values from -100 to 100
- cand_keys: bfloat16 [4, 32, 8, 128], P('groups', 'ctx', 'tp'), may hold values from -4 to 4
- candidate_values: bfloat16 [4, 32, 8, 128], P('groups', 'ctx', 'tp'), may hold values from -5 to 5
- cached_prompt_keys: bfloat16 [256, 128, 8, 128], P(('groups', 'ctx'), None, 'tp'), may hold values from -4 to 4
- cached_prompt_values: bfloat16 [256, 128, 8, 128], P(('groups', 'ctx'), None, 'tp'), may hold values from -5 to 5
- block_lists: int32 [4, 128], P('groups'), may hold values from 0 to 255, as said below
- out_weight: bfloat16 [8192, 8192], P('tp', 'ctx'), may hold values from -0.0625 to 0.0625
Outputs:
- verified: bfloat16 [4, 32, 8192], P('groups', 'tp', 'ctx')
Inputs may be any that keep to these rules, and one draw needn't show every extreme that they name: `block_lists`: each row holds 128 distinct block numbers in increasing order; among blocks 16 * c to 16 * (c + 1) - 1 a row has at most 16 entries, exactly 16 for some c in every row; all rows together have at most 40 entries in one such range, exactly 40 in some.
All inputs are finite; a program needn't handle non-finite values.
Results may differ from a plain program's by a relative error of at most 0.022.
Values may be sent and summed in bfloat16 or wider, within the bound.
A program may use at most 128 MiB of HBM per device.

v0:
```python
import jax
import jax.numpy as jnp
from jax import lax
from jax.sharding import PartitionSpec as P

NEGATIVE = -1e30


def masked_softmax(scores, visible):
    scores = jnp.where(visible, scores, NEGATIVE)
    maxima = jnp.max(scores, axis=-1)
    weights = jnp.where(visible, jnp.exp(scores - maxima[..., None]), 0.0)
    return (weights, maxima, jnp.sum(weights, axis=-1))


def heads_last(stats):
    kv_count, query_group_width, row_count = stats.shape
    return jnp.transpose(stats, (2, 0, 1)).reshape(row_count, kv_count * query_group_width)


def block_terms(query_matrix, block_keys, block_values, visible, factor):
    row_count, kv_count, query_group_width, head_size = query_matrix.shape
    scores = (
        jnp.einsum("nkgd,mkd->kgnm", query_matrix, block_keys, preferred_element_type=jnp.float32)
        * factor
    )
    weights, maxima, denominator = masked_softmax(scores, visible)
    numerator = jnp.einsum(
        "kgnm,mkd->nkgd",
        weights.astype(jnp.bfloat16),
        block_values,
        preferred_element_type=jnp.float32,
    )
    return (
        numerator.reshape(row_count, kv_count * query_group_width, head_size),
        heads_last(maxima),
        heads_last(denominator),
    )


def join_parts(first, second):
    maxima = jnp.maximum(first[1], second[1])
    left_scale = jnp.exp(first[1] - maxima)
    right_scale = jnp.exp(second[1] - maxima)
    numerator = first[0] * left_scale[..., None] + second[0] * right_scale[..., None]
    return (numerator, maxima, first[2] * left_scale + second[2] * right_scale)


def sources_merge(parts):
    numerator, maxima, denominator = parts
    highest = jnp.max(maxima, axis=2)
    rescale = jnp.exp(maxima - highest[:, :, None])
    return (
        jnp.sum(numerator * rescale[..., None], axis=2),
        highest,
        jnp.sum(denominator * rescale, axis=2),
    )


def on_device(
    queries,
    cand_keys,
    candidate_values,
    cached_prompt_keys,
    cached_prompt_values,
    block_lists,
    out_weight,
):
    cand_count, tok_rows, head_local, head_size = queries.shape
    kv_local = cand_keys.shape[2]
    query_group_width = head_local // kv_local
    blocks_here, block_tokens = (cached_prompt_keys.shape[0], cached_prompt_keys.shape[1])
    selected = block_lists.shape[1]
    ranges = lax.axis_size("ctx")
    device = lax.axis_index("ctx")
    cand_length = tok_rows * ranges
    factor = head_size ** (-0.5)
    capacity = min(blocks_here, 4 * selected // ranges)
    lowest = device * blocks_here
    below = jnp.sum((block_lists < lowest).astype(jnp.int32), axis=1)
    inside = jnp.sum((block_lists < lowest + blocks_here).astype(jnp.int32), axis=1) - below
    slot_ids = jnp.arange(capacity)
    where_listed = jnp.clip(below[:, None] + slot_ids[None, :], 0, selected - 1)
    slot_live = slot_ids[None, :] < inside[:, None]
    local_index = jnp.where(
        slot_live, jnp.take_along_axis(block_lists, where_listed, axis=1) - lowest, 0
    )
    gathered_keys = jnp.take(cached_prompt_keys, local_index, axis=0).reshape(
        cand_count, capacity * block_tokens, kv_local, head_size
    )
    gathered_values = jnp.take(cached_prompt_values, local_index, axis=0).reshape(
        cand_count, capacity * block_tokens, kv_local, head_size
    )
    key_live = jnp.repeat(slot_live, block_tokens, axis=1)
    shard_rows = lax.all_gather(queries, "ctx", axis=1, tiled=True)
    row_count = shard_rows.shape[1]
    grouped_queries = shard_rows.reshape(
        cand_count, row_count, kv_local, query_group_width, head_size
    )
    terms = lax.map(
        lambda parts: block_terms(parts[0], parts[1], parts[2], parts[3], factor),
        (grouped_queries, gathered_keys, gathered_values, key_live),
    )
    prompt_parts = tuple((fresh for fresh in terms))
    candidate_own_keys, own_values = (
        lax.all_gather(cand_keys, "ctx", axis=1, tiled=True),
        lax.all_gather(candidate_values, "ctx", axis=1, tiled=True),
    )
    query_pos = device * tok_rows + jnp.arange(tok_rows)
    causal = jnp.arange(cand_length)[None, :] <= query_pos[:, None]
    grouped_local = queries.reshape(cand_count, tok_rows, kv_local, query_group_width, head_size)
    own_scores = (
        jnp.einsum(
            "jnkgd,jmkd->jkgnm",
            grouped_local,
            candidate_own_keys,
            preferred_element_type=jnp.float32,
        )
        * factor
    )
    own_weights, own_max, own_sum = masked_softmax(own_scores, causal)
    own_numer = jnp.einsum(
        "jkgnm,jmkd->jnkgd",
        own_weights.astype(jnp.bfloat16),
        own_values,
        preferred_element_type=jnp.float32,
    )
    own_part = (
        own_numer.reshape(cand_count, tok_rows, head_local, head_size),
        jnp.transpose(own_max, (0, 3, 1, 2)).reshape(cand_count, tok_rows, head_local),
        jnp.transpose(own_sum, (0, 3, 1, 2)).reshape(cand_count, tok_rows, head_local),
    )
    merged = sources_merge(
        (
            lax.all_to_all(
                prompt_parts[0][:, :, None].astype(jnp.bfloat16),
                "ctx",
                split_axis=1,
                concat_axis=2,
                tiled=True,
            ).astype(jnp.float32),
            lax.all_to_all(
                prompt_parts[1][:, :, None].astype(jnp.bfloat16),
                "ctx",
                split_axis=1,
                concat_axis=2,
                tiled=True,
            ).astype(jnp.float32),
            lax.all_to_all(
                prompt_parts[2][:, :, None].astype(jnp.bfloat16),
                "ctx",
                split_axis=1,
                concat_axis=2,
                tiled=True,
            ).astype(jnp.float32),
        )
    )
    numerator, unused_max, denominator = join_parts(merged, own_part)
    attention = (
        (numerator / denominator[..., None])
        .reshape(cand_count, tok_rows, head_local * head_size)
        .astype(jnp.bfloat16)
    )
    partial_value = jnp.einsum(
        "jnf,fc->jnc",
        lax.all_gather(attention, "ctx", axis=1, tiled=True),
        out_weight,
        preferred_element_type=jnp.float32,
    )
    return lax.psum_scatter(
        partial_value.astype(jnp.bfloat16), "tp", scatter_dimension=1, tiled=True
    )


def solution(mesh):
    placed = (
        P("groups", "ctx", "tp", None),
        P("groups", "ctx", "tp", None),
        P("groups", "ctx", "tp", None),
        P(("groups", "ctx"), None, "tp", None),
        P(("groups", "ctx"), None, "tp", None),
        P("groups", None),
        P("tp", "ctx"),
    )
    return jax.shard_map(
        on_device, mesh=mesh, in_specs=placed, out_specs=P("groups", "tp", "ctx"), check_vma=False
    )
```

profile of v0, /device:TPU:0, one launch (start us, length us, event | category | flops | bytes accessed | tf_op | source)
XLA Modules:
  0.0 323.0 jit_solution(12083824224312323788)
XLA Ops:
  10.1 9.3 %gather_fusion.1 = bf16[64,128,4,128]{3,2,1,0:T(4,128)(2,1)} fusion(bf16[16,128,4,128]{3,2,1,0:T(4,128)(2,1)S(1)} %copy-done, s32[1024]{0:T(1024)S(1)} %pad_clamp_fusion), kind=kCustom, calls=%fused_computation.clone | custom fusion | bytes 16777472 | tf_op jit(solution)/shard_map/jit(_take)/gather | solution.py:91
  19.4 10.9 %gather_fusion.2 = bf16[64,128,4,128]{3,2,1,0:T(4,128)(2,1)} fusion(bf16[16,128,4,128]{3,2,1,0:T(4,128)(2,1)} %param.14, s32[1024]{0:T(1024)S(1)} %pad_clamp_fusion), kind=kCustom, calls=%fused_computation.1.clone | custom fusion | bytes 16777472 | tf_op jit(solution)/shard_map/jit(_take)/gather | solution.py:88
  30.4 14.7 %copy_select_fusion = (bf16[4,16,128,4,128]{4,2,1,3,0:T(8,128)(2,1)}, bf16[4,16,128,4,128]{4,2,1,3,0:T(8,128)(2,1)}) fusion(bf16[4,16,128,4,128]{4,3,2,1,0:T(4,128)(2,1)} %bitcast.150, pred[4,16]{1,0:T(4,128)(4,1)S(1)} %get-tuple-element.82, bf16[4,16,128,4,128]{4,3,2,1,0:T(4,128)(2,1)} %bitcast.149), kind=kLoop, calls=%fused_computation.27 | loop fusion | flops 8388608 | bytes 33554496 | tf_op jit(solution)/shard_map/jit(_take)/select_n | solution.py:88
  45.1 22.6 %all-gather.3.cloned.1.call-done = bf16[4,32,32,128]{3,2,1,0:T(8,128)(2,1)} async-done(((bf16[4,2,32,128]{3,2,1,0:T(8,128)(2,1)}), bf16[4,32,32,128]{3,2,1,0:T(8,128)(2,1)}) %all-gather.3.cloned.1.call-update) | async-done | bytes 1048592 | tf_op jit(solution)/shard_map/all_gather | solution.py:95
  69.4 61.6 %while.14 = (s32[]{:T(128)}, bf16[4,32,32,128]{3,2,0,1:T(8,128)(2,1)}, bf16[4,32,32]{2,0,1:T(4,128)(2,1)S(1)}, bf16[4,32,32]{2,0,1:T(4,128)(2,1)S(1)}, bf16[4,20...) while((s32[]{:T(128)}, ...), condition=%wide.region_5.7_spmd, body=%wide.region_2.6_spmd.sunk | while | flops 1101002752 | bytes 64022668 | solution.py:100
  72.5 3.2 copy-done.1
  78.1 5.7 %fusion.58 = bf16[4,128,8,32]{1,3,2,0:T(8,128)(2,1)S(1)} fusion(f32[4,2048,32,8]{1,2,3,0:T(8,128)} %copy-done.1, f32[4,8,32]{2,1,0:T(8,128)S(1)} %get-tuple-element.148, pred[2048]{0:T(1024)(128)(4,1)S(1)} %dynamic-slice_reduce_fusion.2, bf16[4,2048,4,128]{3,1,2,0:T(8,128)(2,1)} %get-tuple-element.173, s32[]{:T(128)} %get-tuple-element.159), kind=kOutput, calls=%fused_computation.10.clone.1 | convolution fusion | flops 547356672 | bytes 10768896 | tf_op jit(solution)/shard_map/while/body/eval_jaxpr/kgnm,mkd->nkgd/dot_general | solution.py:28
  87.9 3.2 copy-done.1
  93.5 5.7 %fusion.58 = bf16[4,128,8,32]{1,3,2,0:T(8,128)(2,1)S(1)} fusion(f32[4,2048,32,8]{1,2,3,0:T(8,128)} %copy-done.1, f32[4,8,32]{2,1,0:T(8,128)S(1)} %get-tuple-element.148, pred[2048]{0:T(1024)(128)(4,1)S(1)} %dynamic-slice_reduce_fusion.2, bf16[4,2048,4,128]{3,1,2,0:T(8,128)(2,1)} %get-tuple-element.173, s32[]{:T(128)} %get-tuple-element.159), kind=kOutput, calls=%fused_computation.10.clone.1 | convolution fusion | flops 547356672 | bytes 10768896 | tf_op jit(solution)/shard_map/while/body/eval_jaxpr/kgnm,mkd->nkgd/dot_general | solution.py:28
  103.3 3.2 copy-done.1
  108.9 5.7 %fusion.58 = bf16[4,128,8,32]{1,3,2,0:T(8,128)(2,1)S(1)} fusion(f32[4,2048,32,8]{1,2,3,0:T(8,128)} %copy-done.1, f32[4,8,32]{2,1,0:T(8,128)S(1)} %get-tuple-element.148, pred[2048]{0:T(1024)(128)(4,1)S(1)} %dynamic-slice_reduce_fusion.2, bf16[4,2048,4,128]{3,1,2,0:T(8,128)(2,1)} %get-tuple-element.173, s32[]{:T(128)} %get-tuple-element.159), kind=kOutput, calls=%fused_computation.10.clone.1 | convolution fusion | flops 547356672 | bytes 10768896 | tf_op jit(solution)/shard_map/while/body/eval_jaxpr/kgnm,mkd->nkgd/dot_general | solution.py:28
  115.7 3.0 bitcast_reduce_fusion.2
  118.7 3.2 copy-done.1
  124.3 5.7 %fusion.58 = bf16[4,128,8,32]{1,3,2,0:T(8,128)(2,1)S(1)} fusion(f32[4,2048,32,8]{1,2,3,0:T(8,128)} %copy-done.1, f32[4,8,32]{2,1,0:T(8,128)S(1)} %get-tuple-element.148, pred[2048]{0:T(1024)(128)(4,1)S(1)} %dynamic-slice_reduce_fusion.2, bf16[4,2048,4,128]{3,1,2,0:T(8,128)(2,1)} %get-tuple-element.173, s32[]{:T(128)} %get-tuple-element.159), kind=kOutput, calls=%fused_computation.10.clone.1 | convolution fusion | flops 547356672 | bytes 10768896 | tf_op jit(solution)/shard_map/while/body/eval_jaxpr/kgnm,mkd->nkgd/dot_general | solution.py:28
  131.8 4.5 %all-to-all-start.2 = ((bf16[16,2,128]{2,1,0:T(2,128)(2,1)}), bf16[16,2,128]{2,1,0:T(2,128)(2,1)S(1)}, u32[]{:S(2)}, u32[]{:S(2)}) async-start(bf16[16,2,128]{2,1,0:T(2,128)(2,1)} %reshape.228), calls=%async_computation.2 | async-start | bytes 16384 | tf_op jit(solution)/shard_map/all_to_all | solution.py:149
  136.4 7.1 %all-to-all-done.2 = bf16[16,2,128]{2,1,0:T(2,128)(2,1)S(1)} async-done(((bf16[16,2,128]{2,1,0:T(2,128)(2,1)}), bf16[16,2,128]{2,1,0:T(2,128)(2,1)S(1)}, u32[]{:S(2)}, u32[]{:S(2)}) %all-to-all-start.2) | async-done | bytes 8224 | tf_op jit(solution)/shard_map/all_to_all | solution.py:149
  143.5 9.9 %all_to_all.33 = bf16[16,2,128]{2,1,0:T(2,128)(2,1)S(1)} all-to-all(bf16[16,2,128]{2,1,0:T(2,128)(2,1)S(1)} %reshape.226), channel_id=1, replica_groups=mesh['groups'=1,'ctx'=16,'tp'=2] {'ctx'}, dimensions={0} | all-to-all | bytes 16384 | tf_op jit(solution)/shard_map/all_to_all | solution.py:142
  153.4 3.7 %all-to-all-start = ((bf16[4,32,1,32,128]{4,3,0,2,1:T(8,128)(2,1)}), bf16[4,32,1,32,128]{4,3,0,2,1:T(8,128)(2,1)S(1)}, u32[]{:S(2)}, u32[]{:S(2)}) async-start(bf16[4,32,1,32,128]{4,3,0,2,1:T(8,128)(2,1)} %bitcast.156), calls=%async_computation | async-start | bytes 2097152 | tf_op jit(solution)/shard_map/all_to_all | solution.py:135
  157.1 47.7 %all_gather.13 = bf16[4,32,4,128]{3,2,0,1:T(4,128)(2,1)S(1)} all-gather(bf16[4,2,4,128]{3,2,0,1:T(4,128)(2,1)S(1)} %copy.77), channel_id=1, replica_groups=mesh['groups'=1,'ctx'=16,'tp'=2] {'ctx'}, dimensions={1}, use_global_device_ids=true | all-gather | bytes 139264 | tf_op jit(solution)/shard_map/all_gather | solution.py:106
  205.6 38.1 %all_gather.14 = bf16[4,32,4,128]{3,2,0,1:T(4,128)(2,1)S(1)} all-gather(bf16[4,2,4,128]{3,2,0,1:T(4,128)(2,1)S(1)} %copy.82), channel_id=1, replica_groups=mesh['groups'=1,'ctx'=16,'tp'=2] {'ctx'}, dimensions={1}, use_global_device_ids=true | all-gather | bytes 139264 | tf_op jit(solution)/shard_map/all_gather | solution.py:107
  248.7 3.9 %fusion.22 = f32[4,2,32,128]{3,1,2,0:T(2,128)S(1)} fusion(f32[4,16,2,1,32,128]{5,4,0,2,1,3:T(8,128)S(1)} %convert.23, f32[4,2,16,32]{1,2,3,0:T(8,128)} %copy.76), kind=kLoop, calls=%fused_computation.32 | loop fusion | flops 1015808 | bytes 2244608 | tf_op jit(solution)/shard_map/reduce_sum | solution.py:54
  254.5 51.1 %all-gather.5.cloned.1.call-done = bf16[4,32,4096]{2,0,1:T(4,128)(2,1)} async-done(((bf16[4,2,4096]{2,0,1:T(4,128)(2,1)}), bf16[4,32,4096]{2,0,1:T(4,128)(2,1)}) %all-gather.5.cloned.1.call-update) | async-done | bytes 1048592 | tf_op jit(solution)/shard_map/all_gather | solution.py:166
  305.5 4.4 %fusion.23 = bf16[4,32,512]{2,1,0:T(8,128)(2,1)} fusion(bf16[4096,512]{1,0:T(8,128)(2,1)} %param.17, bf16[4,32,4096]{2,0,1:T(4,128)(2,1)} %all-gather.5.cloned.1.call-done), kind=kOutput, calls=%fused_computation.33 | convolution fusion | flops 536936448 | bytes 5373952 | tf_op jit(solution)/shard_map/jnf,fc->jnc/dot_general | solution.py:164
  309.9 6.6 %reduce-scatter.2.cloned.1.call-done = bf16[4,16,512]{2,1,0:T(8,128)(2,1)} async-done(((bf16[4,32,512]{2,1,0:T(8,128)(2,1)}), bf16[4,16,512]{2,1,0:T(8,128)(2,1)}) %reduce-scatter.2.cloned.1.call-update) | async-done | bytes 65552 | tf_op jit(solution)/shard_map/reduce_scatter | solution.py:170
  (99 shorter events, 36.4 us)
Async XLA Ops:
  6.5 3.6 %copy-start = (bf16[16,128,4,128]{3,2,1,0:T(4,128)(2,1)S(1)}, bf16[16,128,4,128]{3,2,1,0:T(4,128)(2,1)}, u32[]{:S(2)}) copy-start(bf16[16,128,4,128]{3,2,1,0:T(4,128)(2,1)} %param.15) | copy-start | bytes 6291460
  6.5 61.2 %all-gather.3.cloned.1.call-start = ((), (), s32[]{:S(2)}) async-start(), calls=%async_computation.4 | async-start | bytes 1114112 | tf_op jit(solution)/shard_map/all_gather | solution.py:95
  69.4 87.7 %copy-start.3 = (bf16[4,2,4,128]{3,2,1,0:T(4,128)(2,1)S(1)}, bf16[4,2,4,128]{3,2,1,0:T(4,128)(2,1)}, u32[]{:S(2)}) copy-start(bf16[4,2,4,128]{3,2,1,0:T(4,128)(2,1)} %param.12) | copy-start | bytes 24580
  69.4 135.5 %copy-start.2 = (bf16[4,2,32,128]{3,2,1,0:T(8,128)(2,1)S(1)}, bf16[4,2,32,128]{3,2,1,0:T(8,128)(2,1)}, u32[]{:S(2)}) copy-start(bf16[4,2,32,128]{3,2,1,0:T(8,128)(2,1)} %param.11) | copy-start | bytes 196612
  69.4 136.2 %copy-start.4 = (bf16[4,2,4,128]{3,2,1,0:T(4,128)(2,1)S(1)}, bf16[4,2,4,128]{3,2,1,0:T(4,128)(2,1)}, u32[]{:S(2)}) copy-start(bf16[4,2,4,128]{3,2,1,0:T(4,128)(2,1)} %param.13) | copy-start | bytes 24580
  72.5 3.2 copy-start.1
  87.9 3.2 copy-start.1
  103.3 3.2 copy-start.1
  118.7 3.2 copy-start.1
  131.8 11.7 %all-to-all-start.2 = ((bf16[16,2,128]{2,1,0:T(2,128)(2,1)}), bf16[16,2,128]{2,1,0:T(2,128)(2,1)S(1)}, u32[]{:S(2)}, u32[]{:S(2)}) async-start(bf16[16,2,128]{2,1,0:T(2,128)(2,1)} %reshape.228), calls=%async_computation.2 | async-start | bytes 16384 | tf_op jit(solution)/shard_map/all_to_all | solution.py:149
  153.4 95.1 %all-to-all-start = ((bf16[4,32,1,32,128]{4,3,0,2,1:T(8,128)(2,1)}), bf16[4,32,1,32,128]{4,3,0,2,1:T(8,128)(2,1)S(1)}, u32[]{:S(2)}, u32[]{:S(2)}) async-start(bf16[4,32,1,32,128]{4,3,0,2,1:T(8,128)(2,1)} %bitcast.156), calls=%async_computation | async-start | bytes 2097152 | tf_op jit(solution)/shard_map/all_to_all | solution.py:135
  157.0 148.5 %all-gather.5.cloned.1.call-start = ((), (), s32[]{:S(2)}) async-start(), calls=%async_computation.5 | async-start | bytes 1114112 | tf_op jit(solution)/shard_map/all_gather | solution.py:166
  254.4 62.1 %reduce-scatter.2.cloned.1.call-start = ((), (), s32[]{:S(2)}) async-start(), calls=%async_computation.6 | async-start | bytes 196608 | tf_op jit(solution)/shard_map/reduce_scatter | solution.py:170
Sparse Core Ops, SparseCore 0:
  10.1 57.6 all-gather.2
  254.5 50.9 all-gather.4
  310.0 6.4 reduce-scatter.1
where the time goes:
time: 324 us; the launch traced here: 323 us
  blocking collectives  95.6 us (30%)
  waiting for transfers between devices  88.1 us (27%)
  local copies, waits for them, and re-layouts  47.6 us (15%)
  matrix products  39.7 us (12%)
  other arithmetic  30.1 us (9%)
  between operations  13.4 us (4%)
  starting transfers between devices  8.24 us (3%)
    all_gather x1, waiting for transfers between devices, on_device(): lax.all_gather(attention, 'ctx', axis=1, tiled=True)  51.1 us
    all_gather x1, blocking collectives, on_device(): lax.all_gather(cand_keys, 'ctx', axis=1, tiled=True)  47.7 us
    all_gather x1, blocking collectives, on_device(): lax.all_gather(candidate_values, 'ctx', axis=1, tiled=True)  38.1 us
    dot_general x4, matrix products, block_terms(): jnp.einsum('kgnm,mkd->nkgd', weights.astype(jnp.bfloat16), block_values,...  22.9 us
    all_gather x1, waiting for transfers between devices, on_device(): shard_rows = lax.all_gather(queries, 'ctx', axis=1, tiled=True)  22.6 us
    select_n x1, other arithmetic, on_device(): jnp.take(cached_prompt_keys, local_index, axis=0)  14.7 us
    while x8, local copies, waits for them, and re-layouts  12.9 us
    dot_general x4, matrix products, block_terms(): jnp.einsum('nkgd,mkd->kgnm', query_matrix, block_keys, preferred_element_...  12 us
  transfers between devices with their start and end apart: 5, of which 4 were waited for; matrix products, arithmetic and copies ran while one was open for 13% of the time, Pallas kernels for 0%

commit v1 on v0

v1 whole, which is shorter than its diff:
```python
import functools
import math

import jax
import jax.numpy as jnp
from jax import lax
from jax.experimental import pallas as pl
from jax.experimental.pallas import tpu as pltpu
from jax.sharding import PartitionSpec as P

NEGATIVE = -1e30
MESH = pl.DeviceIdType.MESH
F32, BF16 = jnp.float32, jnp.bfloat16


class Place:
    def __init__(self, ranges):
        self.me = lax.axis_index("ctx")
        self.depth = ranges // 4
        self.x, self.y, self.z = self.me % 2, (self.me // 2) % 2, self.me // 4
        self.beside_x = self.at(self.z, self.y, 1 - self.x)
        self.beside_y = self.at(self.z, 1 - self.y, self.x)

    def at(self, z, y, x):
        return z * 4 + y * 2 + x

    def shifted(self, d):
        return (self.z + d + self.depth) % self.depth

    def line(self, d):
        return self.at(self.shifted(d), self.y, self.x)


def greet(place, with_tp):
    barrier = pltpu.get_barrier_semaphore()
    others = [place.line(d) for d in range(1, place.depth)]
    for other in others + [place.beside_x, place.beside_y]:
        pl.semaphore_signal(barrier, inc=1, device_id={"ctx": other}, device_id_type=MESH)
    if with_tp:
        pl.semaphore_signal(
            barrier, inc=1, device_id={"tp": 1 - lax.axis_index("tp")}, device_id_type=MESH
        )
    pl.semaphore_wait(barrier, place.depth + 1 + int(with_tp))


def gather_pieces(place, buf, send, recv):
    def copy(kind, d, owner, target):
        return pltpu.make_async_remote_copy(
            src_ref=buf.at[owner],
            dst_ref=buf.at[owner],
            send_sem=send.at[kind, d],
            recv_sem=recv.at[kind, d],
            device_id={"ctx": target},
            device_id_type=MESH,
        )

    sent = []

    def go(*what):
        one = copy(*what)
        one.start()
        sent.append(one)

    depth = place.depth
    z_of = [place.shifted(-d) for d in range(depth)]

    def spread(d):
        owner = place.at(z_of[d], place.y, place.x)
        if d:
            copy(0, d, owner, place.me).wait_recv()
        go(1, d, owner, place.beside_x)
        go(2, d, owner, place.beside_y)

    def relay(d):
        from_x = place.at(z_of[d], place.y, 1 - place.x)
        from_y = place.at(z_of[d], 1 - place.y, place.x)
        copy(1, d, from_x, place.me).wait_recv()
        if d % 2 == 0:
            go(3, d, from_x, place.beside_y)
        copy(2, d, from_y, place.me).wait_recv()
        if d % 2 == 1:
            go(3, d, from_y, place.beside_x)

    for d in range(1, depth):
        go(0, d, place.me, place.line(d))
    spread(0)
    for d in range(1, depth):
        spread(d)
        relay(d - 1)
    relay(depth - 1)
    for d in range(depth):
        copy(3, d, place.at(z_of[d], 1 - place.y, 1 - place.x), place.me).wait_recv()
    for one in sent:
        one.wait_send()


def query_kernel(ranges, q_ref, out_ref, send, recv):
    place = Place(ranges)
    out_ref[place.me] = q_ref[...]
    greet(place, False)
    gather_pieces(place, out_ref, send, recv)


def attend_kernel(
    sizes,
    lists_smem,
    lists_ref,
    q_ref,
    own_k_ref,
    own_v_ref,
    k_ref,
    v_ref,
    out_ref,
    wide,
    k_heads,
    v_heads,
    scores,
    sums,
    acc,
    top,
):
    cands, toks, kv, group, blocks, block_tokens, head, tile_owners = sizes
    chunk = pl.program_id(0)
    me = lax.axis_index("ctx")
    scale = head ** (-0.5) * math.log2(math.e)
    rows = tile_owners * toks * group
    lowest = me * blocks

    @pl.when(chunk == 0)
    def _():
        def spread(b, carry):
            for src, dst in ((k_ref, k_heads), (v_ref, v_heads)):
                wide[...] = src[b].astype(F32)
                for h in range(kv):
                    dst[h, b] = wide[pl.ds(h, block_tokens, stride=kv), :].astype(BF16)
            return carry

        lax.fori_loop(0, blocks, spread, 0)

    row = lax.broadcasted_iota(jnp.int32, (rows, block_tokens), 0)
    lane = lax.broadcasted_iota(jnp.int32, (rows, block_tokens), 1)
    query_pos = chunk * tile_owners * toks + row // group
    own_seen = (lane < toks) & (me * toks + lane <= query_pos)
    stats = jnp.zeros((rows, 128), F32)
    lanes = lax.broadcasted_iota(jnp.int32, (rows, 128), 1)
    nt = (((1,), (1,)), ((), ()))
    for j in range(cands):
        line = lists_ref[j : j + 1, :]
        below = jnp.sum((line < lowest).astype(jnp.int32))
        count = jnp.sum((line < lowest + blocks).astype(jnp.int32)) - below
        last = lists_smem.shape[1] - 1

        def pair_of(i):
            first = lists_smem[j, jnp.minimum(below + 2 * i, last)] - lowest
            second = lists_smem[j, jnp.minimum(below + 2 * i + 1, last)] - lowest
            inside = 2 * i + 1 < count
            return first, jnp.where(inside, second, first), inside

        queries = []
        for h in range(kv):
            q = q_ref[:, j, :, h * group : (h + 1) * group, :].astype(F32)
            queries.append(q.reshape(rows, head).astype(BF16))
            own = lax.dot_general(
                queries[h], own_k_ref[h, j], nt, preferred_element_type=F32
            )
            own = jnp.where(own_seen, own, NEGATIVE)
            sums[h] = own
            top[h] = own

        def first_pass(i, carry):
            a, b, inside = pair_of(i)
            for h in range(kv):
                keys = jnp.concatenate([k_heads[h, a], k_heads[h, b]], axis=0)
                s = lax.dot_general(queries[h], keys, nt, preferred_element_type=F32)
                left = s[:, :block_tokens]
                right = jnp.where(inside, s[:, block_tokens:], NEGATIVE)
                scores[h, i, :, :block_tokens] = left
                scores[h, i, :, block_tokens:] = right
                top[h] = jnp.maximum(top[h], jnp.maximum(left, right))
            return carry

        pairs = (count + 1) // 2
        lax.fori_loop(0, pairs, first_pass, 0)
        for h in range(kv):
            peak = jnp.max(top[h], axis=1, keepdims=True).astype(BF16).astype(F32)
            p = jnp.where(own_seen, jnp.exp2((sums[h] - peak) * scale), 0.0)
            sums[h] = p
            acc[h] = jnp.dot(p.astype(BF16), own_v_ref[h, j], preferred_element_type=F32)
            top[h] = jnp.broadcast_to(peak, (rows, block_tokens))

        def second_pass(i, carry):
            a, b, _ = pair_of(i)
            for h in range(kv):
                values = jnp.concatenate([v_heads[h, a], v_heads[h, b]], axis=0)
                peak = top[h]
                left = jnp.exp2((scores[h, i, :, :block_tokens] - peak) * scale)
                right = jnp.exp2((scores[h, i, :, block_tokens:] - peak) * scale)
                sums[h] += left + right
                p = jnp.concatenate([left.astype(BF16), right.astype(BF16)], axis=1)
                acc[h] += jnp.dot(p, values, preferred_element_type=F32)
            return carry

        lax.fori_loop(0, pairs, second_pass, 0)
        for h in range(kv):
            combo = h * cands + j
            total = jnp.sum(sums[h], axis=1, keepdims=True)
            stats = jnp.where(lanes == combo, top[h], stats)
            stats = jnp.where(lanes == 64 + combo, total, stats)
            per = toks * group
            out_ref[:, combo * per : (combo + 1) * per, :] = (
                acc[h].reshape(tile_owners, per, head).astype(BF16)
            )
    per = toks * group
    full = kv * cands * per
    out_ref[:, full : full + per, :] = stats.reshape(tile_owners, per, 128).astype(BF16)


def merge(pieces, combos, per, scale):
    full = combos * per
    stats = [load(full, per).astype(F32) for load in pieces]
    peak = functools.reduce(jnp.maximum, stats)
    low = lax.broadcasted_iota(jnp.int32, (per, 128), 1) < 64
    scales = [jnp.exp2((jnp.where(low, s - peak, 0.0)) * scale) for s in stats]
    total = sum(pltpu.roll(w, 64, 1) * s for w, s in zip(scales, stats))
    sums = []
    for c in range(combos):
        sums.append(
            sum(
                load(c * per, per).astype(F32) * w[:, c : c + 1]
                for load, w in zip(pieces, scales)
            )
        )
    return sums, jnp.where(low, peak, total), total


def finish_kernel(
    ranges,
    sizes,
    parts_ref,
    weight_ref,
    out_ref,
    from_diag,
    from_x,
    from_y,
    from_line,
    to_diag,
    to_line,
    gathered,
    ordered,
    weight,
    total,
    away,
    arrived,
    weight_sem,
    red_send,
    red_recv,
    send,
    recv,
    tp_sems,
):
    cands, toks, kv, group, head = sizes
    place = Place(ranges)
    depth = place.depth
    per = toks * group
    combos = kv * cands
    scale = head ** (-0.5) * math.log2(math.e)
    fetch = pltpu.make_async_copy(weight_ref, weight, weight_sem)
    fetch.start()
    greet(place, True)

    sent = []

    def copy(kind, d, src, dst, target):
        return pltpu.make_async_remote_copy(
            src_ref=src,
            dst_ref=dst,
            send_sem=red_send.at[kind, d],
            recv_sem=red_recv.at[kind, d],
            device_id={"ctx": target},
            device_id_type=MESH,
        )

    def go(*what):
        one = copy(*what)
        one.start()
        sent.append(one)

    def arrive(kind, d, dst):
        copy(kind, d, dst, dst, place.me).wait_recv()

    def owner(d, flip_y, flip_x):
        y = 1 - place.y if flip_y else place.y
        x = 1 - place.x if flip_x else place.x
        return place.at(place.shifted(d), y, x)

    def loader(ref, *index):
        return lambda start, size: ref[(*index, pl.ds(start, size), slice(None))]

    def put(dst, d, sums, stats):
        for c in range(combos):
            dst[d, c * per : (c + 1) * per, :] = sums[c].astype(BF16)
        dst[d, combos * per : (combos + 1) * per, :] = stats.astype(BF16)

    order = list(range(1, depth)) + [0]
    for d in order:
        far = parts_ref.at[owner(d, 1, 1)]
        if d % 2 == 0:
            go(0, d, far, from_diag.at[d], place.beside_x)
        else:
            go(0, d, far, from_diag.at[d], place.beside_y)
    for d in order:
        if d % 2 == 0:
            go(1, d, parts_ref.at[owner(d, 0, 1)], from_x.at[d], place.beside_x)
        else:
            go(2, d, parts_ref.at[owner(d, 1, 0)], from_y.at[d], place.beside_y)
    for d in order:
        arrive(0, d, from_diag.at[d])
        mine = owner(d, 1, 0) if d % 2 == 0 else owner(d, 0, 1)
        sums, stats, _ = merge(
            (loader(parts_ref, mine), loader(from_diag, d)), combos, per, scale
        )
        put(to_diag, d, sums, stats)
        if d % 2 == 0:
            go(2, d, to_diag.at[d], from_y.at[d], place.beside_y)
        else:
            go(1, d, to_diag.at[d], from_x.at[d], place.beside_x)
    for d in order:
        arrive(1, d, from_x.at[d])
        arrive(2, d, from_y.at[d])
        sums, stats, _ = merge(
            (loader(parts_ref, owner(d, 0, 0)), loader(from_x, d), loader(from_y, d)),
            combos,
            per,
            scale,
        )
        put(to_line, d, sums, stats)
        if d:
            go(3, d, to_line.at[d], from_line.at[d], place.line(d))
    for d in range(1, depth):
        arrive(3, d, from_line.at[d])
    sums, _, denominator = merge(
        [loader(to_line, 0)] + [loader(from_line, d) for d in range(1, depth)],
        combos,
        per,
        scale,
    )
    denominator = pltpu.roll(denominator, 64, 1)
    for c in range(combos):
        ordered[c * per : (c + 1) * per, :] = sums[c] / denominator[:, c : c + 1]
    tokens = cands * toks
    for h in range(kv):
        block = [
            ordered[pl.ds(h * tokens * group + g, tokens, stride=group), :] for g in range(group)
        ]
        gathered[place.me, h * tokens * group : (h + 1) * tokens * group, :] = jnp.concatenate(
            block, axis=0
        ).astype(BF16)
    gather_pieces(place, gathered, send, recv)
    fetch.wait()
    total[...] = jnp.zeros_like(total)

    def project(i, carry):
        start = pl.multiple_of(i * 2 * tokens, 2 * tokens)
        both = gathered[:, pl.ds(start, 2 * tokens), :].astype(F32)
        left = both[:, :tokens, :].reshape(ranges * tokens, head).astype(BF16)
        right = both[:, tokens:, :].reshape(ranges * tokens, head).astype(BF16)
        rows = pl.multiple_of(i * 2 * head, 2 * head)
        total[...] += jnp.dot(
            jnp.concatenate([left, right], axis=1),
            weight[pl.ds(rows, 2 * head), :],
            preferred_element_type=F32,
        )
        return carry

    lax.fori_loop(0, kv * group // 2, project, 0)
    half = ranges * tokens // 2
    tp = lax.axis_index("tp")
    away[...] = total[pl.ds(pl.multiple_of((1 - tp) * half, half), half), :].astype(BF16)
    swap = pltpu.make_async_remote_copy(
        src_ref=away,
        dst_ref=arrived,
        send_sem=tp_sems.at[0],
        recv_sem=tp_sems.at[1],
        device_id={"tp": 1 - tp},
        device_id_type=MESH,
    )
    swap.start()
    for one in sent:
        one.wait_send()
    swap.wait()
    mine = total[pl.ds(pl.multiple_of(tp * half, half), half), :]
    out_ref[...] = (mine + arrived[...].astype(F32)).astype(BF16)


def on_device(
    queries,
    cand_keys,
    candidate_values,
    cached_prompt_keys,
    cached_prompt_values,
    block_lists,
    out_weight,
):
    cands, toks, heads, head = queries.shape
    kv = cand_keys.shape[2]
    group = heads // kv
    blocks, block_tokens = cached_prompt_keys.shape[:2]
    ranges = lax.axis_size("ctx")
    depth = ranges // 4
    piece = cands * toks * heads
    per = toks * group
    vmem = pl.BlockSpec(memory_space=pltpu.VMEM)
    limit = 60 * 1024 * 1024

    everyone = pl.pallas_call(
        functools.partial(query_kernel, ranges),
        out_shape=jax.ShapeDtypeStruct((ranges, piece, head), BF16),
        in_specs=[vmem],
        out_specs=vmem,
        scratch_shapes=[
            pltpu.SemaphoreType.DMA((4, depth)),
            pltpu.SemaphoreType.DMA((4, depth)),
        ],
        compiler_params=pltpu.CompilerParams(collective_id=0, has_side_effects=True),
        name="query_gather",
    )(queries.reshape(piece, head))

    tile_owners = min(ranges, 256 // per)
    rows = tile_owners * per
    own = [
        jnp.pad(
            jnp.transpose(a, (2, 0, 1, 3)), ((0, 0), (0, 0), (0, block_tokens - toks), (0, 0))
        )
        for a in (cand_keys, candidate_values)
    ]
    whole = lambda shape: pl.BlockSpec(
        shape, lambda i, *_: (0,) * len(shape), pipeline_mode=pl.Buffered(1)
    )
    own_spec = whole((kv, cands, block_tokens, head))
    cache_spec = whole((blocks, block_tokens * kv, head))
    sizes = (cands, toks, kv, group, blocks, block_tokens, head, tile_owners)
    parts = pl.pallas_call(
        functools.partial(attend_kernel, sizes),
        out_shape=jax.ShapeDtypeStruct((ranges, piece + per, head), BF16),
        grid_spec=pltpu.PrefetchScalarGridSpec(
            num_scalar_prefetch=1,
            grid=(ranges // tile_owners,),
            in_specs=[
                whole(block_lists.shape),
                pl.BlockSpec(
                    (tile_owners, cands, toks, heads, head), lambda i, *_: (i, 0, 0, 0, 0)
                ),
                own_spec,
                own_spec,
                cache_spec,
                cache_spec,
            ],
            out_specs=pl.BlockSpec((tile_owners, piece + per, head), lambda i, *_: (i, 0, 0)),
            scratch_shapes=[
                pltpu.VMEM((block_tokens * kv, head), F32),
                pltpu.VMEM((kv, blocks, block_tokens, head), BF16),
                pltpu.VMEM((kv, blocks, block_tokens, head), BF16),
                pltpu.VMEM((kv, (blocks + 1) // 2, rows, 2 * block_tokens), F32),
                pltpu.VMEM((kv, rows, block_tokens), F32),
                pltpu.VMEM((kv, rows, head), F32),
                pltpu.VMEM((kv, rows, block_tokens), F32),
            ],
        ),
        compiler_params=pltpu.CompilerParams(vmem_limit_bytes=limit),
        name="attend",
    )(
        block_lists,
        block_lists,
        everyone.reshape(ranges, cands, toks, heads, head),
        *own,
        cached_prompt_keys.reshape(blocks, block_tokens * kv, head),
        cached_prompt_values.reshape(blocks, block_tokens * kv, head),
    )

    columns = out_weight.shape[1]
    tokens = cands * toks
    half = ranges * tokens // 2
    block = pltpu.VMEM((depth, piece + per, head), BF16)
    result = pl.pallas_call(
        functools.partial(finish_kernel, ranges, (cands, toks, kv, group, head)),
        out_shape=jax.ShapeDtypeStruct((half, columns), BF16),
        in_specs=[vmem, pl.BlockSpec(memory_space=pl.ANY)],
        out_specs=vmem,
        scratch_shapes=[block] * 6
        + [
            pltpu.VMEM((ranges, piece, head), BF16),
            pltpu.VMEM((piece, head), F32),
            pltpu.VMEM(out_weight.shape, BF16),
            pltpu.VMEM((2 * half, columns), F32),
            pltpu.VMEM((half, columns), BF16),
            pltpu.VMEM((half, columns), BF16),
            pltpu.SemaphoreType.DMA,
            pltpu.SemaphoreType.DMA((4, depth)),
            pltpu.SemaphoreType.DMA((4, depth)),
            pltpu.SemaphoreType.DMA((4, depth)),
            pltpu.SemaphoreType.DMA((4, depth)),
            pltpu.SemaphoreType.DMA((2,)),
        ],
        compiler_params=pltpu.CompilerParams(
            collective_id=1, has_side_effects=True, vmem_limit_bytes=limit
        ),
        name="reduce_project",
    )(parts, out_weight)
    result = result.reshape(ranges // 2, cands, toks, columns)
    return jnp.transpose(result, (1, 0, 2, 3)).reshape(cands, ranges * toks // 2, columns)


def solution(mesh):
    placed = (
        P("groups", "ctx", "tp", None),
        P("groups", "ctx", "tp", None),
        P("groups", "ctx", "tp", None),
        P(("groups", "ctx"), None, "tp", None),
        P(("groups", "ctx"), None, "tp", None),
        P("groups", None),
        P("tp", "ctx"),
    )
    return jax.shard_map(
        on_device, mesh=mesh, in_specs=placed, out_specs=P("groups", "tp", "ctx"), check_vma=False
    )
```

time: 324 us -> 88.1 us (0.27)
  blocking collectives: 95.6 us -> 0 us
  waiting for transfers between devices: 88.1 us -> 0 us
  Pallas kernels: 0 us -> 83.7 us
  local copies, waits for them, and re-layouts: 47.6 us -> 4.8 us
  matrix products: 39.7 us -> 0 us
  other arithmetic: 30.1 us -> 0 us
  between operations: 13.4 us -> 0.03 us
  starting transfers between devices: 8.24 us -> 0 us
    all_gather x2 -> x0, blocking collectives: 85.8 us -> none  [the longest x1 47.7 us: on_device(): lax.all_gather(cand_keys, 'ctx', axis=1, tiled=True)]
    pallas_call x0 -> x3, Pallas kernels: none -> 83.7 us  [the longest x1 41.4 us: on_device(): pl.pallas_call(functools.partial(finish_kernel, ranges, (cands, toks, kv,...]
    all_gather x2 -> x0, waiting for transfers between devices: 73.7 us -> none  [the longest x1 51.1 us: on_device(): lax.all_gather(attention, 'ctx', axis=1, tiled=True)]
    dot_general x11 -> x0, matrix products: 39.7 us -> none  [the longest x4 22.9 us: block_terms(): jnp.einsum('kgnm,mkd->nkgd', weights.astype(jnp.bfloat16), block_values,...]
    gather x5 -> x0, local copies, waits for them, and re-layouts: 22 us -> none  [the longest x1 10.9 us: on_device(): jnp.take(cached_prompt_keys, local_index, axis=0)]
    select_n x1 -> x0, other arithmetic: 14.7 us -> none  [on_device(): jnp.take(cached_prompt_keys, local_index, axis=0)]
    reduce_sum x7 -> x0, other arithmetic: 13.7 us -> none  [the longest x5 9.02 us: masked_softmax(): return (weights, maxima, jnp.sum(weights, axis=-1))]
    while x8 -> x0, local copies, waits for them, and re-layouts: 12.9 us -> none
  transfers between devices with their start and end apart: 5 -> 0, of which waited for: 4 -> 0; matrix products, arithmetic and copies ran while one was open for 13% -> 0% of each run, Pallas kernels for 0% -> 0%
where the time goes in v1:
time: 88.1 us; the launch traced here: 88.6 us
  Pallas kernels  83.7 us (95%)
  local copies, waits for them, and re-layouts  4.8 us (5%)
    pallas_call x1, Pallas kernels, on_device(): pl.pallas_call(functools.partial(finish_kernel, ranges, (cands, toks, kv,...  41.4 us
    pallas_call x1, Pallas kernels, on_device(): pl.pallas_call(functools.partial(query_kernel, ranges), out_shape=jax.Sha...  24 us
    pallas_call x1, Pallas kernels, on_device(): pl.pallas_call(functools.partial(attend_kernel, sizes), out_shape=jax.Sha...  18.3 us
    pad x2, local copies, waits for them, and re-layouts, on_device(): jnp.pad(jnp.transpose(a, (2, 0, 1, 3)), ((0, 0), (0, 0), (0, block_tokens...  1.81 us

profile of v1, /device:TPU:0, one launch (start us, length us, event | category | flops | bytes accessed | tf_op | source)
XLA Modules:
  0.0 88.6 jit_solution(1940318306092691633)
XLA Ops:
  0.0 0.7 copy.14
  0.7 0.7 copy.13
  1.4 0.9 %pad.8.own_v_ref = bf16[4,4,128,128]{3,2,1,0:T(8,128)(2,1)} pad(bf16[4,4,2,128]{3,2,1,0:T(2,128)(2,1)S(1)} %bitcast.17, bf16[]{:T(256)} %constant.2.clone.1), padding=0_0x0_0x0_126x0_0 | pad | bytes 532482 | tf_op jit(solution)/shard_map/jit(_pad)/pad | solution.py:431
  2.3 0.9 %pad.7.own_k_ref = bf16[4,4,128,128]{3,2,1,0:T(8,128)(2,1)} pad(bf16[4,4,2,128]{3,2,1,0:T(2,128)(2,1)S(1)} %bitcast.16, bf16[]{:T(256)} %constant.2.clone.1), padding=0_0x0_0x0_126x0_0 | pad | bytes 532482 | tf_op jit(solution)/shard_map/jit(_pad)/pad | solution.py:431
  3.2 24.0 %query_gather.1 = bf16[16,256,128]{2,1,0:T(8,128)(2,1)} custom-call(bf16[256,128]{1,0:T(8,128)(2,1)} %bitcast.15), custom_call_target="tpu_custom_call" | custom-call | tf_op jit(solution)/shard_map/query_gather/pallas_call | solution.py:415
  27.3 18.3 %attend.1.parts_ref = bf16[16,272,128]{2,1,0:T(8,128)(2,1)} custom-call(s32[4,128]{1,0:T(4,128)} %lists_ref.1, s32[4,128]{1,0:T(4,128)} %lists_ref.1, bf16[16,4,2,32,128]{4,3,2,1,0:T(8,128)(2,1)} %bitcast.11, bf16[4,4,128,128]{3,2,1,0:T(8,128)(2,1)} %pad.7.own_k_ref, bf16[4,4,128,128]{3,2,1,0:T(8,128)(2,1)} %pad.8.own_v_ref, bf16[16,512,128]{2,1,0:T(8,128)(2,1)} %bitcast.12, ...), custom_call_target="tpu_custom_call" | custom-call | tf_op jit(solution)/shard_map/attend/pallas_call | solution.py:442
  45.6 41.4 %reduce_project.1 = bf16[64,512]{1,0:T(8,128)(2,1)} custom-call(bf16[16,272,128]{2,1,0:T(8,128)(2,1)} %attend.1.parts_ref, bf16[4096,512]{1,0:T(8,128)(2,1)} %weight_ref.1), custom_call_target="tpu_custom_call" | custom-call | tf_op jit(solution)/shard_map/reduce_project/pallas_call | solution.py:484
  87.0 0.9 reshape.22
  87.9 0.7 reshape.23
  (1 shorter events, 0.0 us)

commit v2 on v1

v2 whole, which is shorter than its diff:
```python
import functools
import math

import jax
import jax.numpy as jnp
from jax import lax
from jax.experimental import pallas as pl
from jax.experimental.pallas import tpu as pltpu
from jax.sharding import PartitionSpec as P

NEGATIVE = -1e30
MESH = pl.DeviceIdType.MESH
F32, BF16 = jnp.float32, jnp.bfloat16


class Place:
    def __init__(self, ranges):
        self.me = lax.axis_index("ctx")
        self.depth = ranges // 4
        self.x, self.y, self.z = self.me % 2, (self.me // 2) % 2, self.me // 4
        self.beside_x = self.at(self.z, self.y, 1 - self.x)
        self.beside_y = self.at(self.z, 1 - self.y, self.x)

    def at(self, z, y, x):
        return z * 4 + y * 2 + x

    def shifted(self, d):
        return (self.z + d + self.depth) % self.depth

    def line(self, d):
        return self.at(self.shifted(d), self.y, self.x)


def greet(place, with_tp):
    barrier = pltpu.get_barrier_semaphore()
    others = [place.line(d) for d in range(1, place.depth)]
    for other in others + [place.beside_x, place.beside_y]:
        pl.semaphore_signal(barrier, inc=1, device_id={"ctx": other}, device_id_type=MESH)
    if with_tp:
        pl.semaphore_signal(
            barrier, inc=1, device_id={"tp": 1 - lax.axis_index("tp")}, device_id_type=MESH
        )
    pl.semaphore_wait(barrier, place.depth + 1 + int(with_tp))


def near_first(depth):
    order = []
    for step in range(1, depth // 2 + 1):
        order += [step] + ([depth - step] if depth - step != step else [])
    return order


def gather_pieces(place, buf, send, recv, work=lambda step: None):
    def copy(kind, d, half, owner, target):
        return pltpu.make_async_remote_copy(
            src_ref=buf.at[owner, half],
            dst_ref=buf.at[owner, half],
            send_sem=send.at[kind, d, half],
            recv_sem=recv.at[kind, d, half],
            device_id={"ctx": target},
            device_id_type=MESH,
        )

    sent = []

    def go(*what):
        one = copy(*what)
        one.start()
        sent.append(one)

    depth = place.depth
    z_of = [place.shifted(-d) for d in range(depth)]

    def spread(d, half):
        owner = place.at(z_of[d], place.y, place.x)
        if d:
            copy(0, d, half, owner, place.me).wait_recv()
        go(1, d, half, owner, place.beside_x)
        go(2, d, half, owner, place.beside_y)

    def relay(d, half):
        from_x = place.at(z_of[d], place.y, 1 - place.x)
        from_y = place.at(z_of[d], 1 - place.y, place.x)
        if half == 0:
            copy(1, d, half, from_x, place.me).wait_recv()
            go(3, d, half, from_x, place.beside_y)
        else:
            copy(2, d, half, from_y, place.me).wait_recv()
            go(3, d, half, from_y, place.beside_x)

    def settle(d, half):
        from_x = place.at(z_of[d], place.y, 1 - place.x)
        from_y = place.at(z_of[d], 1 - place.y, place.x)
        if half == 0:
            copy(2, d, half, from_y, place.me).wait_recv()
        else:
            copy(1, d, half, from_x, place.me).wait_recv()
        across = place.at(z_of[d], 1 - place.y, 1 - place.x)
        copy(3, d, half, across, place.me).wait_recv()

    order = near_first(depth)
    for half in range(2):
        spread(0, half)
    for d in order:
        for half in range(2):
            go(0, d, half, place.me, place.line(d))
    work(0)
    steps = [(d, half) for d in [0] + order for half in range(2)]
    for i, step in enumerate(steps):
        if i + 2 < len(steps):
            spread(*steps[i + 2])
        relay(*step)
        work(i + 1)
    for step in steps:
        settle(*step)
    for one in sent:
        one.wait_send()


def query_kernel(
    ranges,
    kv,
    q_ref,
    k_ref,
    v_ref,
    out_ref,
    k_out,
    v_out,
    raw,
    wide,
    heads,
    send,
    recv,
    in_sems,
    out_sems,
):
    place = Place(ranges)
    sources, results = (k_ref, v_ref), (k_out, v_out)
    fetches = [pltpu.make_async_copy(sources[n], raw.at[n], in_sems.at[n]) for n in range(2)]
    for fetch in fetches:
        fetch.start()
    out_ref[place.me] = q_ref[...]
    greet(place, False)
    blocks, block_tokens = raw.shape[1], raw.shape[2] // kv
    parts = 4
    per = blocks // parts
    stores = []

    def work(step):
        if step >= 2 * parts:
            return
        n, part = step // parts, step % parts
        if part == 0:
            fetches[n].wait()

        def one(b, carry):
            wide[...] = raw[n, b].astype(F32)
            for h in range(kv):
                heads[n, h, b] = wide[pl.ds(h, block_tokens, stride=kv), :].astype(BF16)
            return carry

        lax.fori_loop(part * per, (part + 1) * per, one, 0)
        some = pl.ds(part * per, per)
        store = pltpu.make_async_copy(
            heads.at[n, :, some], results[n].at[:, some], out_sems.at[n, part]
        )
        store.start()
        stores.append(store)

    gather_pieces(place, out_ref, send, recv, work)
    for store in stores:
        store.wait()


def attend_kernel(
    sizes,
    lists_smem,
    lists_ref,
    q_ref,
    own_k_ref,
    own_v_ref,
    k_ref,
    v_ref,
    out_ref,
    k_heads,
    v_heads,
    scores,
    sums,
    acc,
    top,
    sems,
):
    cands, toks, kv, group, blocks, block_tokens, head, tile_owners = sizes
    chunk = pl.program_id(0)
    me = lax.axis_index("ctx")
    scale = head ** (-0.5) * math.log2(math.e)
    rows = tile_owners * toks * group
    lowest = me * blocks

    fetch_k = pltpu.make_async_copy(k_ref, k_heads, sems.at[0])
    fetch_v = pltpu.make_async_copy(v_ref, v_heads, sems.at[1])

    @pl.when(chunk == 0)
    def _():
        fetch_k.start()
        fetch_v.start()

    key_row = lax.broadcasted_iota(jnp.int32, (block_tokens, head), 0)

    def own_block(ref, h, j):
        rows_here = ref[j].astype(F32)
        block = jnp.zeros((block_tokens, head), F32)
        for t in range(toks):
            block = jnp.where(key_row == t, rows_here[t, h : h + 1, :], block)
        return block.astype(BF16)

    row = lax.broadcasted_iota(jnp.int32, (rows, block_tokens), 0)
    lane = lax.broadcasted_iota(jnp.int32, (rows, block_tokens), 1)
    query_pos = chunk * tile_owners * toks + row // group
    own_seen = (lane < toks) & (me * toks + lane <= query_pos)
    stats = [jnp.zeros((rows, 128), F32)] * 2
    per = toks * group
    lanes = lax.broadcasted_iota(jnp.int32, (rows, 128), 1)
    nt = (((1,), (1,)), ((), ()))
    for j in range(cands):
        line = lists_ref[j : j + 1, :]
        below = jnp.sum((line < lowest).astype(jnp.int32))
        count = jnp.sum((line < lowest + blocks).astype(jnp.int32)) - below
        last = lists_smem.shape[1] - 1

        def pair_of(i):
            first = lists_smem[j, jnp.minimum(below + 2 * i, last)] - lowest
            second = lists_smem[j, jnp.minimum(below + 2 * i + 1, last)] - lowest
            inside = 2 * i + 1 < count
            return first, jnp.where(inside, second, first), inside

        queries = []
        for h in range(kv):
            q = q_ref[:, j, :, h * group : (h + 1) * group, :].astype(F32)
            queries.append(q.reshape(rows, head).astype(BF16))
            own = lax.dot_general(
                queries[h], own_block(own_k_ref, h, j), nt, preferred_element_type=F32
            )
            own = jnp.where(own_seen, own, NEGATIVE)
            sums[h] = own
            top[h] = own

        if j == 0:
            pl.when(chunk == 0)(fetch_k.wait)

        def first_pass(i, carry):
            a, b, inside = pair_of(i)
            for h in range(kv):
                keys = jnp.concatenate([k_heads[h, a], k_heads[h, b]], axis=0)
                s = lax.dot_general(queries[h], keys, nt, preferred_element_type=F32)
                left = s[:, :block_tokens]
                right = jnp.where(inside, s[:, block_tokens:], NEGATIVE)
                scores[h, i, :, :block_tokens] = left
                scores[h, i, :, block_tokens:] = right
                top[h] = jnp.maximum(top[h], jnp.maximum(left, right))
            return carry

        pairs = (count + 1) // 2
        lax.fori_loop(0, pairs, first_pass, 0)
        for h in range(kv):
            peak = jnp.max(top[h], axis=1, keepdims=True).astype(BF16).astype(F32)
            p = jnp.where(own_seen, jnp.exp2((sums[h] - peak) * scale), 0.0)
            sums[h] = p
            acc[h] = jnp.dot(
                p.astype(BF16), own_block(own_v_ref, h, j), preferred_element_type=F32
            )
            top[h] = jnp.broadcast_to(peak, (rows, block_tokens))

        def second_pass(i, carry):
            a, b, _ = pair_of(i)
            for h in range(kv):
                values = jnp.concatenate([v_heads[h, a], v_heads[h, b]], axis=0)
                peak = top[h]
                left = jnp.exp2((scores[h, i, :, :block_tokens] - peak) * scale)
                right = jnp.exp2((scores[h, i, :, block_tokens:] - peak) * scale)
                sums[h] += left + right
                p = jnp.concatenate([left.astype(BF16), right.astype(BF16)], axis=1)
                acc[h] += jnp.dot(p, values, preferred_element_type=F32)
            return carry

        if j == 0:
            pl.when(chunk == 0)(fetch_v.wait)
        lax.fori_loop(0, pairs, second_pass, 0)
        for h in range(kv):
            half, combo = h // (kv // 2), (h % (kv // 2)) * cands + j
            total = jnp.sum(sums[h], axis=1, keepdims=True)
            stats[half] = jnp.where(lanes == combo, top[h], stats[half])
            stats[half] = jnp.where(lanes == 64 + combo, total, stats[half])
            out_ref[:, half, combo * per : (combo + 1) * per, :] = (
                acc[h].reshape(tile_owners, per, head).astype(BF16)
            )
    full = kv // 2 * cands * per
    for half in range(2):
        out_ref[:, half, full : full + per, :] = (
            stats[half].reshape(tile_owners, per, 128).astype(BF16)
        )


def merge(pieces, combos, per, scale):
    full = combos * per
    stats = [load(full, per).astype(F32) for load in pieces]
    peak = functools.reduce(jnp.maximum, stats)
    low = lax.broadcasted_iota(jnp.int32, (per, 128), 1) < 64
    scales = [jnp.exp2((jnp.where(low, s - peak, 0.0)) * scale) for s in stats]
    total = sum(pltpu.roll(w, 64, 1) * s for w, s in zip(scales, stats))
    sums = []
    for c in range(combos):
        sums.append(
            sum(
                load(c * per, per).astype(F32) * w[:, c : c + 1]
                for load, w in zip(pieces, scales)
            )
        )
    return sums, jnp.where(low, peak, total), total


def finish_kernel(
    ranges,
    sizes,
    parts_ref,
    weight_ref,
    out_ref,
    from_diag,
    from_x,
    from_y,
    from_line,
    to_diag,
    to_line,
    gathered,
    ordered,
    weight,
    total,
    away,
    arrived,
    lines,
    weight_sem,
    red_send,
    red_recv,
    send,
    recv,
    tp_sems,
):
    cands, toks, kv, group, head = sizes
    place = Place(ranges)
    depth = place.depth
    per = toks * group
    combos = kv // 2 * cands
    scale = head ** (-0.5) * math.log2(math.e)
    fetch = pltpu.make_async_copy(weight_ref, weight, weight_sem)
    fetch.start()
    greet(place, True)

    sent = []

    def copy(kind, d, half, src, dst, target):
        return pltpu.make_async_remote_copy(
            src_ref=src,
            dst_ref=dst.at[d, half],
            send_sem=red_send.at[kind, d, half],
            recv_sem=red_recv.at[kind, d, half],
            device_id={"ctx": target},
            device_id_type=MESH,
        )

    def go(*what):
        one = copy(*what)
        one.start()
        sent.append(one)

    def arrive(kind, d, half, dst):
        copy(kind, d, half, dst.at[d, half], dst, place.me).wait_recv()

    def owner(d, flip_y, flip_x):
        y = 1 - place.y if flip_y else place.y
        x = 1 - place.x if flip_x else place.x
        return place.at(place.shifted(d), y, x)

    def loader(ref, *index):
        return lambda start, size: ref[(*index, pl.ds(start, size), slice(None))]

    def put(dst, d, half, sums, stats):
        for c in range(combos):
            dst[d, half, c * per : (c + 1) * per, :] = sums[c].astype(BF16)
        dst[d, half, combos * per : (combos + 1) * per, :] = stats.astype(BF16)

    def begin(d):
        go(0, d, 0, parts_ref.at[owner(d, 1, 1), 0], from_diag, place.beside_x)
        go(0, d, 1, parts_ref.at[owner(d, 1, 1), 1], from_diag, place.beside_y)
        go(1, d, 0, parts_ref.at[owner(d, 0, 1), 0], from_x, place.beside_x)
        go(2, d, 1, parts_ref.at[owner(d, 1, 0), 1], from_y, place.beside_y)

    def pass_on(d):
        for half in range(2):
            arrive(0, d, half, from_diag)
            mine = owner(d, 1, 0) if half == 0 else owner(d, 0, 1)
            pieces = (loader(parts_ref, mine, half), loader(from_diag, d, half))
            sums, stats, _ = merge(pieces, combos, per, scale)
            put(to_diag, d, half, sums, stats)
            if half == 0:
                go(2, d, half, to_diag.at[d, half], from_y, place.beside_y)
            else:
                go(1, d, half, to_diag.at[d, half], from_x, place.beside_x)

    def plane(d):
        for half in range(2):
            arrive(1, d, half, from_x)
            arrive(2, d, half, from_y)
            pieces = (
                loader(parts_ref, owner(d, 0, 0), half),
                loader(from_x, d, half),
                loader(from_y, d, half),
            )
            sums, stats, _ = merge(pieces, combos, per, scale)
            put(to_line, d, half, sums, stats)
            if d:
                go(3, d, half, to_line.at[d, half], from_line, place.line(d))

    order = near_first(depth)[::-1] + [0]
    begin(order[0])
    begin(order[1])
    for i, d in enumerate(order):
        pass_on(d)
        if i + 2 < depth:
            begin(order[i + 2])
        if i >= 1:
            plane(order[i - 1])
    plane(order[-1])
    for half in range(2):
        for d in range(1, depth):
            arrive(3, d, half, from_line)
        sums, _, denominator = merge(
            [loader(to_line, 0, half)] + [loader(from_line, d, half) for d in range(1, depth)],
            combos,
            per,
            scale,
        )
        denominator = pltpu.roll(denominator, 64, 1)
        for c in range(combos):
            row = (half * combos + c) * per
            ordered[row : row + per, :] = sums[c] / denominator[:, c : c + 1]
    tokens = cands * toks
    for h in range(kv):
        block = [
            ordered[pl.ds(h * tokens * group + g, tokens, stride=group), :] for g in range(group)
        ]
        half, at = h // (kv // 2), (h % (kv // 2)) * tokens * group
        gathered[place.me, half, at : at + tokens * group, :] = jnp.concatenate(
            block, axis=0
        ).astype(BF16)
    gather_pieces(place, gathered, send, recv)
    fetch.wait()
    total[...] = jnp.zeros_like(total)

    def project(i, carry):
        steps = kv * group // 4
        start = pl.multiple_of((i % steps) * 2 * tokens, 2 * tokens)
        both = gathered[:, i // steps, pl.ds(start, 2 * tokens), :].astype(F32)
        left = both[:, :tokens, :].reshape(ranges * tokens, head).astype(BF16)
        right = both[:, tokens:, :].reshape(ranges * tokens, head).astype(BF16)
        rows = pl.multiple_of(i * 2 * head, 2 * head)
        total[...] += jnp.dot(
            jnp.concatenate([left, right], axis=1),
            weight[pl.ds(rows, 2 * head), :],
            preferred_element_type=F32,
        )
        return carry

    lax.fori_loop(0, kv * group // 2, project, 0)
    half = ranges * tokens // 2
    tp = lax.axis_index("tp")
    away[...] = total[pl.ds(pl.multiple_of((1 - tp) * half, half), half), :].astype(BF16)
    swap = pltpu.make_async_remote_copy(
        src_ref=away,
        dst_ref=arrived,
        send_sem=tp_sems.at[0],
        recv_sem=tp_sems.at[1],
        device_id={"tp": 1 - tp},
        device_id_type=MESH,
    )
    swap.start()
    for one in sent:
        one.wait_send()
    swap.wait()
    mine = total[pl.ds(pl.multiple_of(tp * half, half), half), :]
    columns = total.shape[1]
    joined = mine + arrived[...].astype(F32)
    owners, size = ranges // 2, ranges // 2 * toks
    for c in range(columns // 128):
        lines[c, 0] = joined[:, c * 128 : (c + 1) * 128]
        for j in range(cands):
            for t in range(toks):
                lines[c, 1, pl.ds(j * size + t, owners, stride=toks), :] = lines[
                    c, 0, pl.ds(j * toks + t, owners, stride=tokens), :
                ]
            out_ref[j, :, c * 128 : (c + 1) * 128] = lines[
                c, 1, j * size : (j + 1) * size, :
            ].astype(BF16)


def on_device(
    queries,
    cand_keys,
    candidate_values,
    cached_prompt_keys,
    cached_prompt_values,
    block_lists,
    out_weight,
):
    cands, toks, heads, head = queries.shape
    kv = cand_keys.shape[2]
    group = heads // kv
    blocks, block_tokens = cached_prompt_keys.shape[:2]
    ranges = lax.axis_size("ctx")
    depth = ranges // 4
    piece = cands * toks * heads
    per = toks * group
    vmem = pl.BlockSpec(memory_space=pltpu.VMEM)
    limit = 60 * 1024 * 1024

    anywhere = pl.BlockSpec(memory_space=pl.ANY)
    semaphores = [pltpu.SemaphoreType.DMA((4, depth, 2))] * 2
    cache = (blocks, block_tokens * kv, head)
    sorted_cache = (kv, blocks, block_tokens, head)
    everyone, keys, values = pl.pallas_call(
        functools.partial(query_kernel, ranges, kv),
        out_shape=(
            jax.ShapeDtypeStruct((ranges, 2, piece // 2, head), BF16),
            jax.ShapeDtypeStruct(sorted_cache, BF16),
            jax.ShapeDtypeStruct(sorted_cache, BF16),
        ),
        in_specs=[vmem, anywhere, anywhere],
        out_specs=(vmem, anywhere, anywhere),
        scratch_shapes=[
            pltpu.VMEM((2, *cache), BF16),
            pltpu.VMEM((block_tokens * kv, head), F32),
            pltpu.VMEM((2, *sorted_cache), BF16),
            *semaphores,
            pltpu.SemaphoreType.DMA((2,)),
            pltpu.SemaphoreType.DMA((2, 4)),
        ],
        compiler_params=pltpu.CompilerParams(
            collective_id=0, has_side_effects=True, vmem_limit_bytes=limit
        ),
        name="query_gather",
    )(
        queries.reshape(2, piece // 2, head),
        cached_prompt_keys.reshape(cache),
        cached_prompt_values.reshape(cache),
    )

    tile_owners = min(ranges, 256 // per)
    rows = tile_owners * per
    half_rows = piece // 2 + per
    whole = lambda shape: pl.BlockSpec(
        shape, lambda i, *_: (0,) * len(shape), pipeline_mode=pl.Buffered(1)
    )
    own_spec = whole(cand_keys.shape)
    sizes = (cands, toks, kv, group, blocks, block_tokens, head, tile_owners)
    parts = pl.pallas_call(
        functools.partial(attend_kernel, sizes),
        out_shape=jax.ShapeDtypeStruct((ranges, 2, half_rows, head), BF16),
        grid_spec=pltpu.PrefetchScalarGridSpec(
            num_scalar_prefetch=1,
            grid=(ranges // tile_owners,),
            in_specs=[
                whole(block_lists.shape),
                pl.BlockSpec(
                    (tile_owners, cands, toks, heads, head), lambda i, *_: (i, 0, 0, 0, 0)
                ),
                own_spec,
                own_spec,
                anywhere,
                anywhere,
            ],
            out_specs=pl.BlockSpec((tile_owners, 2, half_rows, head), lambda i, *_: (i, 0, 0, 0)),
            scratch_shapes=[
                pltpu.VMEM((kv, blocks, block_tokens, head), BF16),
                pltpu.VMEM((kv, blocks, block_tokens, head), BF16),
                pltpu.VMEM((kv, (blocks + 1) // 2, rows, 2 * block_tokens), F32),
                pltpu.VMEM((kv, rows, block_tokens), F32),
                pltpu.VMEM((kv, rows, head), F32),
                pltpu.VMEM((kv, rows, block_tokens), F32),
                pltpu.SemaphoreType.DMA((2,)),
            ],
        ),
        compiler_params=pltpu.CompilerParams(vmem_limit_bytes=limit),
        name="attend",
    )(
        block_lists,
        block_lists,
        everyone.reshape(ranges, cands, toks, heads, head),
        cand_keys,
        candidate_values,
        keys,
        values,
    )

    columns = out_weight.shape[1]
    tokens = cands * toks
    half = ranges * tokens // 2
    block = pltpu.VMEM((depth, 2, half_rows, head), BF16)
    return pl.pallas_call(
        functools.partial(finish_kernel, ranges, (cands, toks, kv, group, head)),
        out_shape=jax.ShapeDtypeStruct((cands, ranges * toks // 2, columns), BF16),
        in_specs=[vmem, pl.BlockSpec(memory_space=pl.ANY)],
        out_specs=vmem,
        scratch_shapes=[block] * 6
        + [
            pltpu.VMEM((ranges, 2, piece // 2, head), BF16),
            pltpu.VMEM((piece, head), F32),
            pltpu.VMEM(out_weight.shape, BF16),
            pltpu.VMEM((2 * half, columns), F32),
            pltpu.VMEM((half, columns), BF16),
            pltpu.VMEM((half, columns), BF16),
            pltpu.VMEM((columns // 128, 2, half, 128), F32),
            pltpu.SemaphoreType.DMA,
            *semaphores,
            *semaphores,
            pltpu.SemaphoreType.DMA((2,)),
        ],
        compiler_params=pltpu.CompilerParams(
            collective_id=1, has_side_effects=True, vmem_limit_bytes=limit
        ),
        name="reduce_project",
    )(parts, out_weight)


def solution(mesh):
    placed = (
        P("groups", "ctx", "tp", None),
        P("groups", "ctx", "tp", None),
        P("groups", "ctx", "tp", None),
        P(("groups", "ctx"), None, "tp", None),
        P(("groups", "ctx"), None, "tp", None),
        P("groups", None),
        P("tp", "ctx"),
    )
    return jax.shard_map(
        on_device, mesh=mesh, in_specs=placed, out_specs=P("groups", "tp", "ctx"), check_vma=False
    )
```

time: 88.1 us -> 82 us (0.931); the launches traced: 88.6 us -> 81.5 us
  Pallas kernels: 83.7 us -> 80 us
  local copies, waits for them, and re-layouts: 4.8 us -> 1.47 us
    pad x2 -> x0, local copies, waits for them, and re-layouts: 1.81 us -> none  [on_device(): jnp.pad(jnp.transpose(a, (2, 0, 1, 3)), ((0, 0), (0, 0), (0, block_tokens...]
    pallas_call x1, Pallas kernels: 41.4 us -> 39.7 us  [on_device(): pl.pallas_call(functools.partial(finish_kernel, ranges, (cands, toks, kv,...]
    reshape x2 -> x0, local copies, waits for them, and re-layouts: 1.53 us -> none  [the longest x1 0.87 us: on_device(): result = result.reshape(ranges // 2, cands, toks, columns)]
    pallas_call x1, Pallas kernels: 18.3 us -> 17 us  [on_device(): pl.pallas_call(functools.partial(attend_kernel, sizes), out_shape=jax.Sha...]
where the time goes in v2:
time: 82 us; the launch traced here: 81.5 us
  Pallas kernels  80 us (98%)
  local copies, waits for them, and re-layouts  1.47 us (2%)
    pallas_call x1, Pallas kernels, on_device(): pl.pallas_call(functools.partial(finish_kernel, ranges, (cands, toks, kv,...  39.7 us
    pallas_call x1, Pallas kernels, on_device(): pl.pallas_call(functools.partial(query_kernel, ranges, kv), out_shape=(ja...  23.3 us
    pallas_call x1, Pallas kernels, on_device(): pl.pallas_call(functools.partial(attend_kernel, sizes), out_shape=jax.Sha...  17 us

profile of v2, /device:TPU:0, one launch (start us, length us, event | category | flops | bytes accessed | tf_op | source)
XLA Modules:
  0.0 81.5 jit_solution(3679940387320736494)
XLA Ops:
  0.0 23.3 %query_gather.1 = (bf16[16,2,128,128]{3,2,1,0:T(8,128)(2,1)}, bf16[4,16,128,128]{3,2,1,0:T(8,128)(2,1)}, bf16[4,16,128,128]{3,2,1,0:T(8,128)(2,1)}) custom-call(bf16[2,128,128]{2,1,0:T(8,128)(2,1)} %bitcast.7, bf16[16,512,128]{2,1,0:T(8,128)(2,1)} %bitcast.4, bf16[16,512,128]{2,1,0:T(8,128)(2,1)} %bitcast.5), custom_call_target="tpu_custom_call" | custom-call | tf_op jit(solution)/shard_map/query_gather/pallas_call | solution.py:529
  23.3 17.0 %attend.1.parts_ref = bf16[16,2,144,128]{3,2,1,0:T(8,128)(2,1)} custom-call(s32[4,128]{1,0:T(4,128)} %lists_ref.1, s32[4,128]{1,0:T(4,128)} %lists_ref.1, bf16[16,4,2,32,128]{4,3,2,1,0:T(8,128)(2,1)} %bitcast.6, bf16[4,2,4,128]{3,2,1,0:T(4,128)(2,1)} %own_k_ref.1, bf16[4,2,4,128]{3,2,1,0:T(4,128)(2,1)} %own_v_ref.1, ...), custom_call_target="tpu_custom_call" | custom-call | tf_op jit(solution)/shard_map/attend/pallas_call | solution.py:564
  40.3 39.7 %reduce_project.1 = bf16[4,16,512]{2,1,0:T(8,128)(2,1)} custom-call(bf16[16,2,144,128]{3,2,1,0:T(8,128)(2,1)} %attend.1.parts_ref, bf16[4096,512]{1,0:T(8,128)(2,1)} %weight_ref.1), custom_call_target="tpu_custom_call" | custom-call | tf_op jit(solution)/shard_map/reduce_project/pallas_call | solution.py:607
  80.1 1.5 %copy.9 = bf16[4,16,512]{2,1,0:T(8,128)(2,1)} copy(bf16[4,16,512]{2,1,0:T(8,128)(2,1)} %reduce_project.1) | data formatting | bytes 131072

commit v3 on v2

--- a/solution.py
+++ b/solution.py
@@ -228,11 +228,25 @@
         count = jnp.sum((line < lowest + blocks).astype(jnp.int32)) - below
         last = lists_smem.shape[1] - 1
 
+        def listed(slot):
+            return lists_smem[j, jnp.minimum(below + slot, last)] - lowest
+
+        fours = count // 4
+        pairs = (count - 4 * fours + 1) // 2
+
+        def four_of(i):
+            return 4 * i, [listed(4 * i + n) for n in range(4)], None
+
         def pair_of(i):
-            first = lists_smem[j, jnp.minimum(below + 2 * i, last)] - lowest
-            second = lists_smem[j, jnp.minimum(below + 2 * i + 1, last)] - lowest
-            inside = 2 * i + 1 < count
-            return first, jnp.where(inside, second, first), inside
+            slot = 4 * fours + 2 * i
+            inside = slot + 1 < count
+            first = listed(slot)
+            return slot, [first, jnp.where(inside, listed(slot + 1), first)], inside
+
+        def scores_of(h, picked):
+            keys = jnp.concatenate([k_heads[h, b] for b in picked], axis=0)
+            s = lax.dot_general(queries[h], keys, nt, preferred_element_type=F32)
+            return [s[:, n * block_tokens : (n + 1) * block_tokens] for n in range(len(picked))]
 
         queries = []
         for h in range(kv):
@@ -248,20 +262,17 @@
         if j == 0:
             pl.when(chunk == 0)(fetch_k.wait)
 
-        def first_pass(i, carry):
-            a, b, inside = pair_of(i)
+        def first_pass(pick, i, carry):
+            slot, picked, _ = pick(i)
             for h in range(kv):
-                keys = jnp.concatenate([k_heads[h, a], k_heads[h, b]], axis=0)
-                s = lax.dot_general(queries[h], keys, nt, preferred_element_type=F32)
-                left = s[:, :block_tokens]
-                right = jnp.where(inside, s[:, block_tokens:], NEGATIVE)
-                scores[h, i, :, :block_tokens] = left
-                scores[h, i, :, block_tokens:] = right
-                top[h] = jnp.maximum(top[h], jnp.maximum(left, right))
+                found = scores_of(h, picked)
+                for n, s in enumerate(found):
+                    scores[h, slot + n] = s
+                top[h] = functools.reduce(jnp.maximum, found, top[h])
             return carry
 
-        pairs = (count + 1) // 2
-        lax.fori_loop(0, pairs, first_pass, 0)
+        lax.fori_loop(0, fours, functools.partial(first_pass, four_of), 0)
+        lax.fori_loop(0, pairs, functools.partial(first_pass, pair_of), 0)
         for h in range(kv):
             peak = jnp.max(top[h], axis=1, keepdims=True).astype(BF16).astype(F32)
             p = jnp.where(own_seen, jnp.exp2((sums[h] - peak) * scale), 0.0)
@@ -271,21 +282,25 @@
             )
             top[h] = jnp.broadcast_to(peak, (rows, block_tokens))
 
-        def second_pass(i, carry):
-            a, b, _ = pair_of(i)
+        def second_pass(pick, i, carry):
+            slot, picked, inside = pick(i)
             for h in range(kv):
-                values = jnp.concatenate([v_heads[h, a], v_heads[h, b]], axis=0)
                 peak = top[h]
-                left = jnp.exp2((scores[h, i, :, :block_tokens] - peak) * scale)
-                right = jnp.exp2((scores[h, i, :, block_tokens:] - peak) * scale)
-                sums[h] += left + right
-                p = jnp.concatenate([left.astype(BF16), right.astype(BF16)], axis=1)
-                acc[h] += jnp.dot(p, values, preferred_element_type=F32)
+                p = [
+                    jnp.exp2((scores[h, slot + n] - peak) * scale) for n in range(len(picked))
+                ]
+                if inside is not None:
+                    p[-1] = jnp.where(inside, p[-1], 0.0)
+                sums[h] += functools.reduce(jnp.add, p)
+                values = jnp.concatenate([v_heads[h, b] for b in picked], axis=0)
+                weights = jnp.concatenate([one.astype(BF16) for one in p], axis=1)
+                acc[h] += jnp.dot(weights, values, preferred_element_type=F32)
             return carry
 
         if j == 0:
             pl.when(chunk == 0)(fetch_v.wait)
-        lax.fori_loop(0, pairs, second_pass, 0)
+        lax.fori_loop(0, fours, functools.partial(second_pass, four_of), 0)
+        lax.fori_loop(0, pairs, functools.partial(second_pass, pair_of), 0)
         for h in range(kv):
             half, combo = h // (kv // 2), (h % (kv // 2)) * cands + j
             total = jnp.sum(sums[h], axis=1, keepdims=True)
@@ -581,7 +596,7 @@
             scratch_shapes=[
                 pltpu.VMEM((kv, blocks, block_tokens, head), BF16),
                 pltpu.VMEM((kv, blocks, block_tokens, head), BF16),
-                pltpu.VMEM((kv, (blocks + 1) // 2, rows, 2 * block_tokens), F32),
+                pltpu.VMEM((kv, (blocks + 1) // 2 * 2, rows, block_tokens), F32),
                 pltpu.VMEM((kv, rows, block_tokens), F32),
                 pltpu.VMEM((kv, rows, head), F32),
                 pltpu.VMEM((kv, rows, block_tokens), F32),

time: 82 us -> 79.8 us (0.973); the launches traced: 81.5 us -> 80.2 us
  Pallas kernels: 80 us -> 78.7 us
    pallas_call x1, Pallas kernels: 39.7 us -> 38.4 us  [on_device(): pl.pallas_call(functools.partial(finish_kernel, ranges, (cands, toks, kv,...]
where the time goes in v3:
time: 79.8 us; the launch traced here: 80.2 us
  Pallas kernels  78.7 us (99%)
  local copies, waits for them, and re-layouts  1.47 us (2%)
    pallas_call x1, Pallas kernels, on_device(): pl.pallas_call(functools.partial(finish_kernel, ranges, (cands, toks, kv,...  38.4 us
    pallas_call x1, Pallas kernels, on_device(): pl.pallas_call(functools.partial(query_kernel, ranges, kv), out_shape=(ja...  23.3 us
    pallas_call x1, Pallas kernels, on_device(): pl.pallas_call(functools.partial(attend_kernel, sizes), out_shape=jax.Sha...  16.9 us

profile of v3, /device:TPU:0, one launch (start us, length us, event | category | flops | bytes accessed | tf_op | source)
XLA Modules:
  0.0 80.2 jit_solution(9955167445082672464)
XLA Ops:
  0.0 23.3 %query_gather.1 = (bf16[16,2,128,128]{3,2,1,0:T(8,128)(2,1)}, bf16[4,16,128,128]{3,2,1,0:T(8,128)(2,1)}, bf16[4,16,128,128]{3,2,1,0:T(8,128)(2,1)}) custom-call(bf16[2,128,128]{2,1,0:T(8,128)(2,1)} %bitcast.7, bf16[16,512,128]{2,1,0:T(8,128)(2,1)} %bitcast.4, bf16[16,512,128]{2,1,0:T(8,128)(2,1)} %bitcast.5), custom_call_target="tpu_custom_call" | custom-call | tf_op jit(solution)/shard_map/query_gather/pallas_call | solution.py:544
  23.3 16.9 %attend.1.parts_ref = bf16[16,2,144,128]{3,2,1,0:T(8,128)(2,1)} custom-call(s32[4,128]{1,0:T(4,128)} %lists_ref.1, s32[4,128]{1,0:T(4,128)} %lists_ref.1, bf16[16,4,2,32,128]{4,3,2,1,0:T(8,128)(2,1)} %bitcast.6, bf16[4,2,4,128]{3,2,1,0:T(4,128)(2,1)} %own_k_ref.1, bf16[4,2,4,128]{3,2,1,0:T(4,128)(2,1)} %own_v_ref.1, ...), custom_call_target="tpu_custom_call" | custom-call | tf_op jit(solution)/shard_map/attend/pallas_call | solution.py:579
  40.3 38.4 %reduce_project.1 = bf16[4,16,512]{2,1,0:T(8,128)(2,1)} custom-call(bf16[16,2,144,128]{3,2,1,0:T(8,128)(2,1)} %attend.1.parts_ref, bf16[4096,512]{1,0:T(8,128)(2,1)} %weight_ref.1), custom_call_target="tpu_custom_call" | custom-call | tf_op jit(solution)/shard_map/reduce_project/pallas_call | solution.py:622
  78.7 1.5 %copy.9 = bf16[4,16,512]{2,1,0:T(8,128)(2,1)} copy(bf16[4,16,512]{2,1,0:T(8,128)(2,1)} %reduce_project.1) | data formatting | bytes 131072

commit v4 on v3

--- a/solution.py
+++ b/solution.py
@@ -50,7 +50,7 @@
     return order
 
 
-def gather_pieces(place, buf, send, recv, work=lambda step: None):
+def gather_pieces(place, buf, send, recv, prepare, work=lambda step: None):
     def copy(kind, d, half, owner, target):
         return pltpu.make_async_remote_copy(
             src_ref=buf.at[owner, half],
@@ -100,10 +100,10 @@
 
     order = near_first(depth)
     for half in range(2):
+        prepare(half)
+        for d in order:
+            go(0, d, half, place.me, place.line(d))
         spread(0, half)
-    for d in order:
-        for half in range(2):
-            go(0, d, half, place.me, place.line(d))
     work(0)
     steps = [(d, half) for d in [0] + order for half in range(2)]
     for i, step in enumerate(steps):
@@ -141,6 +141,7 @@
         fetch.start()
     out_ref[place.me] = q_ref[...]
     greet(place, False)
+    prepare = lambda half: None
     blocks, block_tokens = raw.shape[1], raw.shape[2] // kv
     parts = 4
     per = blocks // parts
@@ -167,7 +168,7 @@
         store.start()
         stores.append(store)
 
-    gather_pieces(place, out_ref, send, recv, work)
+    gather_pieces(place, out_ref, send, recv, prepare, work)
     for store in stores:
         store.wait()
 
@@ -445,7 +446,9 @@
         if i >= 1:
             plane(order[i - 1])
     plane(order[-1])
-    for half in range(2):
+    tokens = cands * toks
+
+    def prepare(half):
         for d in range(1, depth):
             arrive(3, d, half, from_line)
         sums, _, denominator = merge(
@@ -458,16 +461,17 @@
         for c in range(combos):
             row = (half * combos + c) * per
             ordered[row : row + per, :] = sums[c] / denominator[:, c : c + 1]
-    tokens = cands * toks
-    for h in range(kv):
-        block = [
-            ordered[pl.ds(h * tokens * group + g, tokens, stride=group), :] for g in range(group)
-        ]
-        half, at = h // (kv // 2), (h % (kv // 2)) * tokens * group
-        gathered[place.me, half, at : at + tokens * group, :] = jnp.concatenate(
-            block, axis=0
-        ).astype(BF16)
-    gather_pieces(place, gathered, send, recv)
+        for n in range(kv // 2):
+            h, at = half * (kv // 2) + n, n * tokens * group
+            block = [
+                ordered[pl.ds(h * tokens * group + g, tokens, stride=group), :]
+                for g in range(group)
+            ]
+            gathered[place.me, half, at : at + tokens * group, :] = jnp.concatenate(
+                block, axis=0
+            ).astype(BF16)
+
+    gather_pieces(place, gathered, send, recv, prepare)
     fetch.wait()
     total[...] = jnp.zeros_like(total)
 

time: 79.8 us -> 80.3 us (level)
    pallas_call x1, Pallas kernels: 16.9 us -> 15 us  [on_device(): pl.pallas_call(functools.partial(attend_kernel, sizes), out_shape=jax.Sha...]
    pallas_call x1, Pallas kernels: 38.4 us -> 40.2 us  [on_device(): pl.pallas_call(functools.partial(finish_kernel, ranges, (cands, toks, kv,...]
where the time goes in v4:
time: 80.3 us; the launch traced here: 80.8 us
  Pallas kernels  79.3 us (99%)
  local copies, waits for them, and re-layouts  1.47 us (2%)
    pallas_call x1, Pallas kernels, on_device(): pl.pallas_call(functools.partial(finish_kernel, ranges, (cands, toks, kv,...  40.2 us
    pallas_call x1, Pallas kernels, on_device(): pl.pallas_call(functools.partial(query_kernel, ranges, kv), out_shape=(ja...  24.1 us
    pallas_call x1, Pallas kernels, on_device(): pl.pallas_call(functools.partial(attend_kernel, sizes), out_shape=jax.Sha...  15 us

profile of v4, /device:TPU:0, one launch (start us, length us, event | category | flops | bytes accessed | tf_op | source)
XLA Modules:
  0.0 80.8 jit_solution(16489359917851331350)
XLA Ops:
  0.0 24.1 %query_gather.1 = (bf16[16,2,128,128]{3,2,1,0:T(8,128)(2,1)}, bf16[4,16,128,128]{3,2,1,0:T(8,128)(2,1)}, bf16[4,16,128,128]{3,2,1,0:T(8,128)(2,1)}) custom-call(bf16[2,128,128]{2,1,0:T(8,128)(2,1)} %bitcast.7, bf16[16,512,128]{2,1,0:T(8,128)(2,1)} %bitcast.4, bf16[16,512,128]{2,1,0:T(8,128)(2,1)} %bitcast.5), custom_call_target="tpu_custom_call" | custom-call | tf_op jit(solution)/shard_map/query_gather/pallas_call | solution.py:548
  24.1 15.0 %attend.1.parts_ref = bf16[16,2,144,128]{3,2,1,0:T(8,128)(2,1)} custom-call(s32[4,128]{1,0:T(4,128)} %lists_ref.1, s32[4,128]{1,0:T(4,128)} %lists_ref.1, bf16[16,4,2,32,128]{4,3,2,1,0:T(8,128)(2,1)} %bitcast.6, bf16[4,2,4,128]{3,2,1,0:T(4,128)(2,1)} %own_k_ref.1, bf16[4,2,4,128]{3,2,1,0:T(4,128)(2,1)} %own_v_ref.1, ...), custom_call_target="tpu_custom_call" | custom-call | tf_op jit(solution)/shard_map/attend/pallas_call | solution.py:583
  39.1 40.2 %reduce_project.1 = bf16[4,16,512]{2,1,0:T(8,128)(2,1)} custom-call(bf16[16,2,144,128]{3,2,1,0:T(8,128)(2,1)} %attend.1.parts_ref, bf16[4096,512]{1,0:T(8,128)(2,1)} %weight_ref.1), custom_call_target="tpu_custom_call" | custom-call | tf_op jit(solution)/shard_map/reduce_project/pallas_call | solution.py:626
  79.3 1.5 %copy.9 = bf16[4,16,512]{2,1,0:T(8,128)(2,1)} copy(bf16[4,16,512]{2,1,0:T(8,128)(2,1)} %reduce_project.1) | data formatting | bytes 131072

commit v5 on v4

--- a/solution.py
+++ b/solution.py
@@ -101,9 +101,9 @@
     order = near_first(depth)
     for half in range(2):
         prepare(half)
+        spread(0, half)
         for d in order:
             go(0, d, half, place.me, place.line(d))
-        spread(0, half)
     work(0)
     steps = [(d, half) for d in [0] + order for half in range(2)]
     for i, step in enumerate(steps):

time: 80.3 us -> 80.7 us (level)
    pallas_call x1, Pallas kernels: 40.2 us -> 39.2 us  [on_device(): pl.pallas_call(functools.partial(finish_kernel, ranges, (cands, toks, kv,...]
where the time goes in v5:
time: 80.7 us; the launch traced here: 80.4 us
  Pallas kernels  78.9 us (98%)
  local copies, waits for them, and re-layouts  1.47 us (2%)
    pallas_call x1, Pallas kernels, on_device(): pl.pallas_call(functools.partial(finish_kernel, ranges, (cands, toks, kv,...  39.2 us
    pallas_call x1, Pallas kernels, on_device(): pl.pallas_call(functools.partial(query_kernel, ranges, kv), out_shape=(ja...  24.1 us
    pallas_call x1, Pallas kernels, on_device(): pl.pallas_call(functools.partial(attend_kernel, sizes), out_shape=jax.Sha...  15.6 us

profile of v5, /device:TPU:0, one launch (start us, length us, event | category | flops | bytes accessed | tf_op | source)
XLA Modules:
  0.0 80.4 jit_solution(17516156039891883812)
XLA Ops:
  0.0 24.1 %query_gather.1 = (bf16[16,2,128,128]{3,2,1,0:T(8,128)(2,1)}, bf16[4,16,128,128]{3,2,1,0:T(8,128)(2,1)}, bf16[4,16,128,128]{3,2,1,0:T(8,128)(2,1)}) custom-call(bf16[2,128,128]{2,1,0:T(8,128)(2,1)} %bitcast.7, bf16[16,512,128]{2,1,0:T(8,128)(2,1)} %bitcast.4, bf16[16,512,128]{2,1,0:T(8,128)(2,1)} %bitcast.5), custom_call_target="tpu_custom_call" | custom-call | tf_op jit(solution)/shard_map/query_gather/pallas_call | solution.py:548
  24.1 15.6 %attend.1.parts_ref = bf16[16,2,144,128]{3,2,1,0:T(8,128)(2,1)} custom-call(s32[4,128]{1,0:T(4,128)} %lists_ref.1, s32[4,128]{1,0:T(4,128)} %lists_ref.1, bf16[16,4,2,32,128]{4,3,2,1,0:T(8,128)(2,1)} %bitcast.6, bf16[4,2,4,128]{3,2,1,0:T(4,128)(2,1)} %own_k_ref.1, bf16[4,2,4,128]{3,2,1,0:T(4,128)(2,1)} %own_v_ref.1, ...), custom_call_target="tpu_custom_call" | custom-call | tf_op jit(solution)/shard_map/attend/pallas_call | solution.py:583
  39.7 39.2 %reduce_project.1 = bf16[4,16,512]{2,1,0:T(8,128)(2,1)} custom-call(bf16[16,2,144,128]{3,2,1,0:T(8,128)(2,1)} %attend.1.parts_ref, bf16[4096,512]{1,0:T(8,128)(2,1)} %weight_ref.1), custom_call_target="tpu_custom_call" | custom-call | tf_op jit(solution)/shard_map/reduce_project/pallas_call | solution.py:626
  79.0 1.5 %copy.9 = bf16[4,16,512]{2,1,0:T(8,128)(2,1)} copy(bf16[4,16,512]{2,1,0:T(8,128)(2,1)} %reduce_project.1) | data formatting | bytes 131072
